TPU v7x, 512 devices: a whole 4x8x8 slice. The times are simulated.
512 devices in a mesh: tensor: 8 (over x, core), context: 64 (over z, y).
Axes of the slice: x: 4, y: 8, z: 8, core: 2. Of those that a mesh axis runs over, the one named last changes fastest.
Arguments:
- token_ids: int32 [2, 6144], P(None, 'context'), may hold values from 0 to 151935
- embed_table: bfloat16 [4096, 151936], P('context', 'tensor')
- input_gain: float32 [4096], replicated, may hold values from 0.1 to 1.9
- w_qkv: bfloat16 [4096, 6144], P('context', 'tensor')
- q_gain: float32 [128], replicated, may hold values from 1 to 10
- k_gain: float32 [128], replicated, may hold values from 1 to 10
Outputs:
- attended: bfloat16 [64, 6144, 128], P('context', 'tensor')
All inputs are finite; a program needn't handle non-finite values.
Results may differ from a plain program's by a relative error of at most 0.0085.
The roundings to bfloat16 on the way count: a program that leaves them out, or rounds other values in their place, can miss the bound.
Values may be sent and summed in bfloat16 or wider, within the bound.
A program may use at most 64 MiB of HBM per device.

v0:
```python
import math
import jax
import jax.numpy as jnp
from jax import lax
from jax.sharding import PartitionSpec as P

QH = 32
KVH = 8
HD = 128
ROPE_BASE = 1000000.0
EPSILON = 1e-06
NEGATIVE = -1e30


def rope_tables(positions, width):
    half_width = width // 2
    exponent = jnp.arange(half_width, dtype=jnp.float32) * (2.0 / width)
    inverse = jnp.exp(-exponent * jnp.log(jnp.float32(ROPE_BASE)))
    angles = positions.astype(jnp.float32)[:, None] * inverse[None, :]
    angles = jnp.concatenate([angles, angles], axis=-1)
    return (jnp.cos(angles), jnp.sin(angles))


def norm_rope(head_vals, head_gain, cos_table, sin_table):
    mean_sq = jnp.mean(head_vals * head_vals, axis=-1, keepdims=True)
    scaled = head_vals * lax.rsqrt(mean_sq + EPSILON) * head_gain
    half_width = scaled.shape[-1] // 2
    rotated = jnp.concatenate([-scaled[..., half_width:], scaled[..., :half_width]], axis=-1)
    return scaled * cos_table[:, None, :] + rotated * sin_table[:, None, :]


def feature_norm(embedded, input_gain):
    hidden = embedded.astype(jnp.float32)
    mean_sq = jnp.mean(hidden * hidden, axis=0, keepdims=True)
    return (hidden * lax.rsqrt(mean_sq + EPSILON) * input_gain[:, None, None]).astype(jnp.bfloat16)


def shards(token_ids, embed_table, input_gain, w_qkv, q_gain, k_gain):
    tensor_count = lax.axis_size("tensor")
    tensor_rank = lax.axis_index("tensor")
    context_rank = lax.axis_index("context")
    seq_count, local_len = token_ids.shape
    width_part, vocab_part = embed_table.shape
    all_ids = lax.all_gather(token_ids, "context", axis=1, tiled=True)
    full_len = all_ids.shape[1]
    local_ids = all_ids - tensor_rank * vocab_part
    inside = (local_ids >= 0) & (local_ids < vocab_part)
    picked = jnp.take(embed_table, jnp.clip(local_ids, 0, vocab_part - 1), axis=1)
    partial_rows = jnp.where(inside[None], picked.astype(jnp.float32), 0.0)
    summed = lax.psum(partial_rows.astype(jnp.bfloat16), "tensor")
    embedded = lax.all_to_all(summed, "context", split_axis=2, concat_axis=0, tiled=True)
    normed = feature_norm(embedded, input_gain)
    projected = jnp.einsum(
        "dsl,dk->slk",
        normed,
        lax.all_gather(w_qkv, "context", axis=0, tiled=True),
        preferred_element_type=jnp.float32,
    )
    joined_proj = lax.all_gather(projected.astype(jnp.bfloat16), "tensor", axis=2, tiled=True)
    positions = context_rank * local_len + jnp.arange(local_len, dtype=jnp.int32)
    cos_table, sin_table = rope_tables(positions, HD)
    wide = joined_proj.astype(jnp.float32)
    queries = norm_rope(
        wide[..., : QH * HD].reshape(seq_count, local_len, QH, HD), q_gain, cos_table, sin_table
    ).astype(jnp.bfloat16)
    key_heads = norm_rope(
        wide[..., QH * HD : (QH + KVH) * HD].reshape(seq_count, local_len, KVH, HD),
        k_gain,
        cos_table,
        sin_table,
    ).astype(jnp.bfloat16)
    values = joined_proj[..., (QH + KVH) * HD :].reshape(seq_count, local_len, KVH, HD)
    group_size = QH // KVH
    queries = jnp.transpose(queries, (0, 2, 1, 3)).reshape(seq_count * QH, local_len, HD)
    key_heads = jnp.repeat(jnp.transpose(key_heads, (0, 2, 1, 3)), group_size, axis=1).reshape(
        seq_count * QH, local_len, HD
    )
    values = jnp.repeat(jnp.transpose(values, (0, 2, 1, 3)), group_size, axis=1).reshape(
        seq_count * QH, local_len, HD
    )
    queries, key_heads, values = (
        lax.all_to_all(queries, "context", split_axis=0, concat_axis=1, tiled=True),
        lax.all_to_all(key_heads, "context", split_axis=0, concat_axis=1, tiled=True),
        lax.all_to_all(values, "context", split_axis=0, concat_axis=1, tiled=True),
    )
    unit_count = queries.shape[0]
    block_rows = full_len // tensor_count
    own_queries = lax.dynamic_slice_in_dim(queries, tensor_rank * block_rows, block_rows, 1)
    query_pos = tensor_rank * block_rows + jnp.arange(block_rows, dtype=jnp.int32)
    query_block = math.gcd(block_rows, 512)
    query_steps = block_rows // query_block
    key_block = math.gcd(full_len, 512)
    key_steps = full_len // key_block
    key_tiles = key_heads.reshape(unit_count, key_steps, key_block, HD)
    value_tiles = values.reshape(unit_count, key_steps, key_block, HD)
    score_scale = HD ** (-0.5)
    outputs = []
    for q_index in range(query_steps):
        query_tile = own_queries[:, q_index * query_block : (q_index + 1) * query_block]
        block_pos = query_pos[q_index * query_block : (q_index + 1) * query_block]
        last_pos = jnp.max(block_pos)

        def key_step(key_index, state_now):
            key_start = key_index * key_block

            def attend(state_in):
                old_max, old_total, old_acc = state_in
                key_tile = lax.dynamic_index_in_dim(key_tiles, key_index, 1, keepdims=False)
                value_tile = lax.dynamic_index_in_dim(value_tiles, key_index, 1, keepdims=False)
                scores = (
                    jnp.einsum(
                        "uqd,ukd->uqk", query_tile, key_tile, preferred_element_type=jnp.float32
                    )
                    * score_scale
                )
                key_pos = key_start + jnp.arange(key_block, dtype=jnp.int32)
                allowed = (key_pos[None, :] <= block_pos[:, None])[None]
                scores = jnp.where(allowed, scores, NEGATIVE)
                new_max = jnp.maximum(old_max, jnp.max(scores, axis=-1))
                weights = jnp.where(allowed, jnp.exp(scores - new_max[..., None]), 0.0)
                shrink = jnp.exp(old_max - new_max)
                new_total = old_total * shrink + jnp.sum(weights, axis=-1)
                new_acc = old_acc * shrink[..., None] + jnp.einsum(
                    "uqk,ukd->uqd",
                    weights.astype(jnp.bfloat16),
                    value_tile,
                    preferred_element_type=jnp.float32,
                )
                return (new_max, new_total, new_acc)

            return lax.cond(key_start <= last_pos, attend, lambda unchanged: unchanged, state_now)

        starting = (
            jnp.full((unit_count, query_block), NEGATIVE, jnp.float32),
            jnp.zeros((unit_count, query_block), jnp.float32),
            jnp.zeros((unit_count, query_block, HD), jnp.float32),
        )
        run_max, run_total, run_acc = lax.fori_loop(0, key_steps, key_step, starting)
        outputs.append((run_acc / run_total[..., None]).astype(jnp.bfloat16))
    attended = jnp.concatenate(outputs, axis=1)
    return attended


def solution(mesh):
    return jax.shard_map(
        shards,
        mesh=mesh,
        in_specs=(
            P(None, "context"),
            P("context", "tensor"),
            P(),
            P("context", "tensor"),
            P(),
            P(),
        ),
        out_specs=P("context", "tensor", None),
        check_vma=False,
    )
```

profile of v0, /device:TPU:15, one launch (start us, length us, event | category | flops | bytes accessed | tf_op | source)
XLA Modules:
  0.0 587.6 jit_solution(8688220472509900719)
XLA Ops:
  7.4 43.1 %all-gather = s32[64,96,2]{1,2,0:T(2,128)S(1)} all-gather(s32[1,96,2]{1,2,0:T(2,128)} %bitcast.203), channel_id=1, replica_groups=mesh['tensor'=8,'context'=64] {'context'}, dimensions={0}, use_global_device_ids=true | all-gather | bytes 49920 | tf_op jit(solution)/shard_map/all_gather | solution.py:44
  50.8 5.8 copy.85
  56.6 1.8 copy.84
  58.5 1.8 copy.83
  60.4 35.7 %gather_fusion = bf16[12288,64]{1,0:T(8,128)(2,1)S(1)} fusion(bf16[64,18992]{0,1:T(8,128)(2,1)} %copy.85, s32[12288]{0:T(1024)S(1)} %broadcast_clamp_fusion), kind=kCustom, calls=%fused_computation | custom fusion | bytes 3194880 | tf_op jit(solution)/shard_map/jit(_take)/gather | solution.py:48
  96.1 29.7 %fusion.58 = bf16[64,2,6144]{0,1,2:T(2,128)(2,1)} fusion(pred[2,6144]{0,1:T(8,128)(4,1)} %copy.84, pred[2,6144]{0,1:T(8,128)(4,1)} %copy.83, bf16[2,6144,64]{2,1,0:T(8,128)(2,1)S(1)} %bitcast.176), kind=kLoop, calls=%fused_computation.77 | loop fusion | flops 3145728 | bytes 3170304 | tf_op jit(solution)/shard_map/convert_element_type | solution.py:50
  126.3 89.1 %all-reduce.2.cloned.1.call-done = bf16[64,2,6144]{0,1,2:T(2,128)(2,1)} async-done(((bf16[64,2,6144]{0,1,2:T(2,128)(2,1)}), bf16[64,2,6144]{0,1,2:T(2,128)(2,1)}) %all-reduce.2.cloned.1.call-update) | async-done | bytes 1572880 | tf_op jit(solution)/shard_map/psum | solution.py:50
  215.4 7.8 %reshape.275 = bf16[64,2,6144]{2,1,0:T(2,128)(2,1)} reshape(bf16[6144,2,64]{2,1,0:T(2,128)(2,1)} %bitcast.179) | data formatting | bytes 3145728
  223.2 12.8 %all-to-all-start = ((bf16[64,2,6144]{2,1,0:T(2,128)(2,1)}), bf16[64,2,6144]{2,1,0:T(2,128)(2,1)S(1)}, u32[]{:S(2)}, u32[]{:S(2)}) async-start(bf16[64,2,6144]{2,1,0:T(2,128)(2,1)} %reshape.275), calls=%async_computation | async-start | bytes 3145728 | tf_op jit(solution)/shard_map/all_to_all | solution.py:51
  236.3 40.8 %all-to-all-done = bf16[64,2,6144]{2,1,0:T(2,128)(2,1)S(1)} async-done(((bf16[64,2,6144]{2,1,0:T(2,128)(2,1)}), bf16[64,2,6144]{2,1,0:T(2,128)(2,1)S(1)}, u32[]{:S(2)}, u32[]{:S(2)}) %all-to-all-start) | async-done | bytes 1572896 | tf_op jit(solution)/shard_map/all_to_all | solution.py:51
  277.1 3.4 reshape.276
  280.5 6.3 %copy.87 = bf16[64,2,6144]{2,0,1:T(8,128)(2,1)S(1)} copy(bf16[64,2,6144]{0,1,2:T(2,128)(2,1)} %bitcast.169) | data formatting | bytes 3145728 | tf_op jit(solution)/shard_map/all_to_all | solution.py:51
  286.8 3.2 reshape.251
  290.1 6.7 %copy.88 = f32[64,64,2,96]{3,1,0,2:T(8,128)} copy(f32[64,64,2,96]{3,0,1,2:T(8,128)} %bitcast.168) | data formatting | bytes 6291456 | tf_op jit(solution)/shard_map/convert_element_type | solution.py:33
  298.5 2.6 fusion.57
  301.2 4.9 fusion.63
  306.5 26.0 %all-gather.6.cloned.1.call-done = bf16[2,96,6144]{2,1,0:T(8,128)(2,1)} async-done(((bf16[2,96,768]{2,1,0:T(8,128)(2,1)}), bf16[2,96,6144]{2,1,0:T(8,128)(2,1)}) %all-gather.6.cloned.1.call-update) | async-done | bytes 2359312 | tf_op jit(solution)/shard_map/all_gather | solution.py:59
  332.5 1.7 slice.57
  339.3 3.0 fusion.62
  342.3 13.1 %all-to-all-start.2 = ((bf16[64,96,128]{2,1,0:T(8,128)(2,1)}), bf16[64,96,128]{2,1,0:T(8,128)(2,1)}, u32[]{:S(2)}, u32[]{:S(2)}) async-start(bf16[64,96,128]{2,1,0:T(8,128)(2,1)} %bitcast.178), calls=%async_computation.2 | async-start | bytes 3145728 | tf_op jit(solution)/shard_map/all_to_all | solution.py:82
  357.2 38.0 %all-to-all-done.2 = bf16[64,96,128]{2,1,0:T(8,128)(2,1)} async-done(((bf16[64,96,128]{2,1,0:T(8,128)(2,1)}), bf16[64,96,128]{2,1,0:T(8,128)(2,1)}, u32[]{:S(2)}, u32[]{:S(2)}) %all-to-all-start.2) | async-done | bytes 1572896 | tf_op jit(solution)/shard_map/all_to_all | solution.py:82
  396.6 8.3 %all-to-all-start.1 = ((bf16[64,96,128]{2,1,0:T(8,128)(2,1)}), bf16[64,96,128]{2,1,0:T(8,128)(2,1)}, u32[]{:S(2)}, u32[]{:S(2)}) async-start(bf16[64,96,128]{2,1,0:T(8,128)(2,1)} %bitcast.177), calls=%async_computation.1 | async-start | bytes 3145728 | tf_op jit(solution)/shard_map/all_to_all | solution.py:83
  405.1 38.4 %all-to-all-done.1 = bf16[64,96,128]{2,1,0:T(8,128)(2,1)} async-done(((bf16[64,96,128]{2,1,0:T(8,128)(2,1)}), bf16[64,96,128]{2,1,0:T(8,128)(2,1)}, u32[]{:S(2)}, u32[]{:S(2)}) %all-to-all-start.1) | async-done | bytes 1572896 | tf_op jit(solution)/shard_map/all_to_all | solution.py:83
  443.5 1.4 broadcast_in_dim.82
  444.9 7.4 %all-to-all-start.3 = ((bf16[64,96,128]{2,1,0:T(8,128)(2,1)}), bf16[64,96,128]{2,1,0:T(8,128)(2,1)S(1)}, u32[]{:S(2)}, u32[]{:S(2)}) async-start(bf16[64,96,128]{2,1,0:T(8,128)(2,1)} %bitcast.44), calls=%async_computation.3 | async-start | bytes 3145728 | tf_op jit(solution)/shard_map/all_to_all | solution.py:84
  453.9 36.7 %all-to-all-done.3 = bf16[64,96,128]{2,1,0:T(8,128)(2,1)S(1)} async-done(((bf16[64,96,128]{2,1,0:T(8,128)(2,1)}), bf16[64,96,128]{2,1,0:T(8,128)(2,1)S(1)}, u32[]{:S(2)}, u32[]{:S(2)}) %all-to-all-start.3) | async-done | bytes 1572896 | tf_op jit(solution)/shard_map/all_to_all | solution.py:84
  490.6 28.7 %while.51 = (s32[]{:T(128)}, f32[1,256]{1,0:T(1,128)S(1)}, f32[1,256]{1,0:T(1,128)S(1)}, f32[1,256,128]{2,1,0:T(8,128)S(1)}, s32[]{:T(128)}, /*index=5*/s32[256]...) while((s32[]{:T(128)}, f32[1,256]{1,0:T(1,128)S(1)}, ...), condition=%wide.region_11.12_spmd, body=%wide.region_6.11_spmd.sunk | while | flops 68748288 | bytes 2190645 | solution.py:138
  491.3 1.8 conditional.6
  493.8 1.8 conditional.6
  496.4 1.8 conditional.6
  498.9 1.8 conditional.6
  501.5 1.8 conditional.6
  504.0 1.8 conditional.6
  506.5 1.8 conditional.6
  509.1 1.8 conditional.6
  511.6 1.8 conditional.6
  514.2 1.8 conditional.6
  516.7 1.8 conditional.6
  519.3 30.0 %while.52 = (s32[]{:T(128)}, f32[1,256]{1,0:T(1,128)S(1)}, f32[1,256]{1,0:T(1,128)S(1)}, f32[1,256,128]{2,1,0:T(8,128)S(1)}, s32[]{:T(128)}, /*index=5*/s32[256]...) while((s32[]{:T(128)}, f32[1,256]{1,0:T(1,128)S(1)}, ...), condition=%wide.region_18.19_spmd, body=%wide.region_13.18_spmd.sunk | while | flops 68748288 | bytes 2190645 | solution.py:138
  520.0 1.8 conditional.7
  522.5 1.8 conditional.7
  525.0 1.8 conditional.7
  527.5 1.8 conditional.7
  530.0 1.8 conditional.7
  532.4 1.8 conditional.7
  534.9 1.8 conditional.7
  537.4 1.8 conditional.7
  539.9 1.8 conditional.7
  542.4 1.8 conditional.7
  544.9 1.8 conditional.7
  547.4 1.8 conditional.7
  549.3 29.9 %while.53 = (s32[]{:T(128)}, f32[1,256]{1,0:T(1,128)S(1)}, f32[1,256]{1,0:T(1,128)S(1)}, f32[1,256,128]{2,1,0:T(8,128)S(1)}, s32[]{:T(128)}, /*index=5*/s32[256]...) while((s32[]{:T(128)}, f32[1,256]{1,0:T(1,128)S(1)}, ...), condition=%wide.region_25.26_spmd, body=%wide.region_20.25_spmd.sunk | while | flops 68748288 | bytes 2190645 | solution.py:138
  550.0 1.8 conditional.8
  552.4 1.8 conditional.8
  554.9 1.8 conditional.8
  557.4 1.8 conditional.8
  559.9 1.8 conditional.8
  562.4 1.8 conditional.8
  564.9 1.8 conditional.8
  567.4 1.8 conditional.8
  569.9 1.8 conditional.8
  572.3 1.8 conditional.8
  574.8 1.8 conditional.8
  577.3 1.8 conditional.8
  (316 shorter events, 77.2 us)
Async XLA Ops:
  7.4 208.0 %all-reduce.2.cloned.1.call-start = ((), (), s32[]{:S(2)}) async-start(), calls=%async_computation.4 | async-start | bytes 6291456 | tf_op jit(solution)/shard_map/psum | solution.py:50
  125.7 175.4 %all-gather.4.cloned.1.call-start = ((), (), s32[]{:S(2)}) async-start(), calls=%async_computation.5 | async-start | bytes 6389760 | tf_op jit(solution)/shard_map/all_gather | solution.py:56
  223.2 53.9 %all-to-all-start = ((bf16[64,2,6144]{2,1,0:T(2,128)(2,1)}), bf16[64,2,6144]{2,1,0:T(2,128)(2,1)S(1)}, u32[]{:S(2)}, u32[]{:S(2)}) async-start(bf16[64,2,6144]{2,1,0:T(2,128)(2,1)} %reshape.275), calls=%async_computation | async-start | bytes 3145728 | tf_op jit(solution)/shard_map/all_to_all | solution.py:51
  236.0 96.5 %all-gather.6.cloned.1.call-start = ((), (), s32[]{:S(2)}) async-start(), calls=%async_computation.6 | async-start | bytes 2654208 | tf_op jit(solution)/shard_map/all_gather | solution.py:59
  297.1 1.4 copy-start.1
  334.8 1.7 copy-start
  336.5 0.7 copy-start.2
  342.3 13.8 %copy-start.3 = (f32[128]{0:T(128)S(1)}, f32[128]{0:T(128)}, u32[]{:S(2)}) copy-start(f32[128]{0:T(128)} %param.23) | copy-start | bytes 1540
  342.3 52.9 %all-to-all-start.2 = ((bf16[64,96,128]{2,1,0:T(8,128)(2,1)}), bf16[64,96,128]{2,1,0:T(8,128)(2,1)}, u32[]{:S(2)}, u32[]{:S(2)}) async-start(bf16[64,96,128]{2,1,0:T(8,128)(2,1)} %bitcast.178), calls=%async_computation.2 | async-start | bytes 3145728 | tf_op jit(solution)/shard_map/all_to_all | solution.py:82
  357.2 47.7 %slice-start = ((bf16[2,96,6144]{2,1,0:T(8,128)(2,1)}), bf16[2,96,1024]{2,1,0:T(8,128)(2,1)S(1)}, s32[]{:S(2)}) async-start(bf16[2,96,6144]{2,1,0:T(8,128)(2,1)} %all-gather.6.cloned.1.call-done), calls=%async_computation.7 | async-start | bytes 786432 | tf_op jit(solution)/shard_map/slice | solution.py:72
  396.6 46.9 %all-to-all-start.1 = ((bf16[64,96,128]{2,1,0:T(8,128)(2,1)}), bf16[64,96,128]{2,1,0:T(8,128)(2,1)}, u32[]{:S(2)}, u32[]{:S(2)}) async-start(bf16[64,96,128]{2,1,0:T(8,128)(2,1)} %bitcast.177), calls=%async_computation.1 | async-start | bytes 3145728 | tf_op jit(solution)/shard_map/all_to_all | solution.py:83
  444.9 45.7 %all-to-all-start.3 = ((bf16[64,96,128]{2,1,0:T(8,128)(2,1)}), bf16[64,96,128]{2,1,0:T(8,128)(2,1)S(1)}, u32[]{:S(2)}, u32[]{:S(2)}) async-start(bf16[64,96,128]{2,1,0:T(8,128)(2,1)} %bitcast.44), calls=%async_computation.3 | async-start | bytes 3145728 | tf_op jit(solution)/shard_map/all_to_all | solution.py:84
Sparse Core Ops, SparseCore 0:
  125.9 89.5 all-reduce.1
  306.3 26.2 all-gather.5
Sparse Core Ops, SparseCore 1:
  129.2 96.6 all-gather.3
where the time goes:
time: 590 us; the launch traced here: 588 us
  waiting for transfers between devices  270 us (46%)
  local copies, waits for them, and re-layouts  81.6 us (14%)
  matrix products  61.3 us (10%)
  other arithmetic  49.3 us (8%)
  blocking collectives  43.1 us (7%)
  starting transfers between devices  41.8 us (7%)
  loops' own time  25.6 us (4%)
  between operations  15.3 us (3%)
    psum x1, waiting for transfers between devices, shards(): summed = lax.psum(partial_rows.astype(jnp.bfloat16), 'tensor')  89.1 us
    all_gather x1, blocking collectives, shards(): all_ids = lax.all_gather(token_ids, 'context', axis=1, tiled=True)  43.1 us
    dot_general x35, matrix products, attend(): jnp.einsum('uqd,ukd->uqk', query_tile, key_tile, preferred_element_type=j...  41.2 us
    all_to_all x1, waiting for transfers between devices, shards(): lax.all_to_all(summed, 'context', split_axis=2, concat_axis=0, tiled=True)  40.8 us
    all_to_all x1, waiting for transfers between devices, shards(): lax.all_to_all(key_heads, 'context', split_axis=0, concat_axis=1, tiled=T...  38.4 us
    all_to_all x1, waiting for transfers between devices, shards(): lax.all_to_all(queries, 'context', split_axis=0, concat_axis=1, tiled=True)  38 us
    all_to_all x1, waiting for transfers between devices, shards(): lax.all_to_all(values, 'context', split_axis=0, concat_axis=1, tiled=True)  36.7 us
    gather x1, local copies, waits for them, and re-layouts, shards(): jnp.take(embed_table, jnp.clip(local_ids, 0, vocab_part - 1), axis=1)  35.7 us
  transfers between devices with their start and end apart: 7, of which 6 were waited for; matrix products, arithmetic and copies ran while one was open for 6% of the time, Pallas kernels for 0%

commit v1 on v0

--- a/solution.py
+++ b/solution.py
@@ -41,7 +41,9 @@
     context_rank = lax.axis_index("context")
     seq_count, local_len = token_ids.shape
     width_part, vocab_part = embed_table.shape
-    all_ids = lax.all_gather(token_ids, "context", axis=1, tiled=True)
+    all_ids = jnp.concatenate(
+        lax.all_to_all(jnp.stack([token_ids] * lax.axis_size("context")), "context", 0, 0), axis=1
+    )
     full_len = all_ids.shape[1]
     local_ids = all_ids - tensor_rank * vocab_part
     inside = (local_ids >= 0) & (local_ids < vocab_part)

time: 590 us -> 556 us (0.942)
  blocking collectives: 43.1 us -> 0 us
  starting transfers between devices: 41.8 us -> 57.9 us
  waiting for transfers between devices: 270 us -> 262 us
    all_gather x1 -> x0, blocking collectives: 43.1 us -> none  [shards(): all_ids = lax.all_gather(token_ids, 'context', axis=1, tiled=True)]
    all_to_all x0 -> x1, starting transfers between devices: none -> 16 us  [shards(): lax.all_to_all(jnp.stack([token_ids] * lax.axis_size('context')), 'contex...]
    psum x1, waiting for transfers between devices: 89.1 us -> 76.9 us  [shards(): summed = lax.psum(partial_rows.astype(jnp.bfloat16), 'tensor')]
  transfers between devices with their start and end apart: 7 -> 8, of which waited for: 6 -> 7; matrix products, arithmetic and copies ran while one was open for 6% -> 7% of each run, Pallas kernels for 0% -> 0%
where the time goes in v1:
time: 556 us; the launch traced here: 554 us
  waiting for transfers between devices  262 us (47%)
  local copies, waits for them, and re-layouts  82.9 us (15%)
  matrix products  61.3 us (11%)
  starting transfers between devices  57.9 us (10%)
  other arithmetic  49.3 us (9%)
  loops' own time  24.8 us (4%)
  between operations  15.3 us (3%)
    psum x1, waiting for transfers between devices, shards(): summed = lax.psum(partial_rows.astype(jnp.bfloat16), 'tensor')  76.9 us
    dot_general x35, matrix products, attend(): jnp.einsum('uqd,ukd->uqk', query_tile, key_tile, preferred_element_type=j...  41.2 us
    all_to_all x1, waiting for transfers between devices, shards(): lax.all_to_all(summed, 'context', split_axis=2, concat_axis=0, tiled=True)  40.8 us
    all_to_all x1, waiting for transfers between devices, shards(): lax.all_to_all(key_heads, 'context', split_axis=0, concat_axis=1, tiled=T...  38.4 us
    all_to_all x1, waiting for transfers between devices, shards(): lax.all_to_all(queries, 'context', split_axis=0, concat_axis=1, tiled=True)  38 us
    all_to_all x1, waiting for transfers between devices, shards(): lax.all_to_all(values, 'context', split_axis=0, concat_axis=1, tiled=True)  36.7 us
    gather x1, local copies, waits for them, and re-layouts, shards(): jnp.take(embed_table, jnp.clip(local_ids, 0, vocab_part - 1), axis=1)  35.7 us
    convert_element_type x1, other arithmetic, shards(): summed = lax.psum(partial_rows.astype(jnp.bfloat16), 'tensor')  29.7 us
  transfers between devices with their start and end apart: 8, of which 7 were waited for; matrix products, arithmetic and copies ran while one was open for 7% of the time, Pallas kernels for 0%

profile of v1, /device:TPU:15, one launch (start us, length us, event | category | flops | bytes accessed | tf_op | source)
XLA Modules:
  0.0 553.6 jit_solution(7496762003331523830)
XLA Ops:
  8.7 16.0 %all-to-all-start = ((s32[64,2,96]{2,1,0:T(2,128)}), s32[64,2,96]{2,1,0:T(2,128)S(1)}, u32[]{:S(2)}, u32[]{:S(2)}) async-start(s32[64,2,96]{2,1,0:T(2,128)} %stack.2), calls=%async_computation | async-start | bytes 131072 | tf_op jit(solution)/shard_map/all_to_all | solution.py:45
  24.8 5.8 %copy.97 = bf16[64,18992]{0,1:T(8,128)(2,1)} copy(bf16[64,18992]{1,0:T(8,128)(2,1)} %param.19) | data formatting | bytes 4861952 | tf_op args[1]
  30.6 4.7 all-to-all-done
  35.7 1.8 copy.95
  37.6 1.8 copy.111
  39.5 35.7 %gather_fusion = bf16[12288,64]{1,0:T(8,128)(2,1)S(1)} fusion(bf16[64,18992]{0,1:T(8,128)(2,1)} %copy.97, s32[12288]{0:T(1024)S(1)} %broadcast_clamp_fusion), kind=kCustom, calls=%fused_computation | custom fusion | bytes 3194880 | tf_op jit(solution)/shard_map/jit(_take)/gather | solution.py:50
  75.2 29.7 %fusion.58 = bf16[64,2,6144]{0,1,2:T(2,128)(2,1)} fusion(pred[2,6144]{0,1:T(8,128)(4,1)} %copy.95, pred[2,6144]{0,1:T(8,128)(4,1)} %bitcast.173, bf16[2,6144,64]{2,1,0:T(8,128)(2,1)S(1)} %bitcast.168), kind=kLoop, calls=%fused_computation.77 | loop fusion | flops 3145728 | bytes 3170304 | tf_op jit(solution)/shard_map/convert_element_type | solution.py:52
  105.4 76.9 %all-reduce.2.cloned.1.call-done = bf16[64,2,6144]{0,1,2:T(2,128)(2,1)} async-done(((bf16[64,2,6144]{0,1,2:T(2,128)(2,1)}), bf16[64,2,6144]{0,1,2:T(2,128)(2,1)}) %all-reduce.2.cloned.1.call-update) | async-done | bytes 1572880 | tf_op jit(solution)/shard_map/psum | solution.py:52
  182.3 7.8 %reshape.311 = bf16[64,2,6144]{2,1,0:T(2,128)(2,1)} reshape(bf16[6144,2,64]{2,1,0:T(2,128)(2,1)} %bitcast.171) | data formatting | bytes 3145728
  190.2 12.8 %all-to-all-start.1 = ((bf16[64,2,6144]{2,1,0:T(2,128)(2,1)}), bf16[64,2,6144]{2,1,0:T(2,128)(2,1)S(1)}, u32[]{:S(2)}, u32[]{:S(2)}) async-start(bf16[64,2,6144]{2,1,0:T(2,128)(2,1)} %reshape.311), calls=%async_computation.1 | async-start | bytes 3145728 | tf_op jit(solution)/shard_map/all_to_all | solution.py:53
  203.2 40.8 %all-to-all-done.1 = bf16[64,2,6144]{2,1,0:T(2,128)(2,1)S(1)} async-done(((bf16[64,2,6144]{2,1,0:T(2,128)(2,1)}), bf16[64,2,6144]{2,1,0:T(2,128)(2,1)S(1)}, u32[]{:S(2)}, u32[]{:S(2)}) %all-to-all-start.1) | async-done | bytes 1572896 | tf_op jit(solution)/shard_map/all_to_all | solution.py:53
  244.0 3.4 reshape.312
  247.4 6.3 %copy.99 = bf16[64,2,6144]{2,0,1:T(8,128)(2,1)S(1)} copy(bf16[64,2,6144]{0,1,2:T(2,128)(2,1)} %bitcast.161) | data formatting | bytes 3145728 | tf_op jit(solution)/shard_map/all_to_all | solution.py:53
  253.7 3.2 reshape.300
  256.9 6.7 %copy.100 = f32[64,64,2,96]{3,1,0,2:T(8,128)} copy(f32[64,64,2,96]{3,0,1,2:T(8,128)} %bitcast.160) | data formatting | bytes 6291456 | tf_op jit(solution)/shard_map/convert_element_type | solution.py:33
  265.4 2.6 fusion.57
  268.1 4.9 fusion.63
  273.4 25.9 %all-gather.5.cloned.1.call-done = bf16[2,96,6144]{2,1,0:T(8,128)(2,1)} async-done(((bf16[2,96,768]{2,1,0:T(8,128)(2,1)}), bf16[2,96,6144]{2,1,0:T(8,128)(2,1)}) %all-gather.5.cloned.1.call-update) | async-done | bytes 2359312 | tf_op jit(solution)/shard_map/all_gather | solution.py:61
  299.3 1.7 slice.57
  306.2 2.9 fusion.62
  309.1 13.1 %all-to-all-start.3 = ((bf16[64,96,128]{2,1,0:T(8,128)(2,1)}), bf16[64,96,128]{2,1,0:T(8,128)(2,1)}, u32[]{:S(2)}, u32[]{:S(2)}) async-start(bf16[64,96,128]{2,1,0:T(8,128)(2,1)} %bitcast.170), calls=%async_computation.3 | async-start | bytes 3145728 | tf_op jit(solution)/shard_map/all_to_all | solution.py:84
  324.1 38.0 %all-to-all-done.3 = bf16[64,96,128]{2,1,0:T(8,128)(2,1)} async-done(((bf16[64,96,128]{2,1,0:T(8,128)(2,1)}), bf16[64,96,128]{2,1,0:T(8,128)(2,1)}, u32[]{:S(2)}, u32[]{:S(2)}) %all-to-all-start.3) | async-done | bytes 1572896 | tf_op jit(solution)/shard_map/all_to_all | solution.py:84
  363.4 8.3 %all-to-all-start.2 = ((bf16[64,96,128]{2,1,0:T(8,128)(2,1)}), bf16[64,96,128]{2,1,0:T(8,128)(2,1)}, u32[]{:S(2)}, u32[]{:S(2)}) async-start(bf16[64,96,128]{2,1,0:T(8,128)(2,1)} %bitcast.169), calls=%async_computation.2 | async-start | bytes 3145728 | tf_op jit(solution)/shard_map/all_to_all | solution.py:85
  371.9 38.4 %all-to-all-done.2 = bf16[64,96,128]{2,1,0:T(8,128)(2,1)} async-done(((bf16[64,96,128]{2,1,0:T(8,128)(2,1)}), bf16[64,96,128]{2,1,0:T(8,128)(2,1)}, u32[]{:S(2)}, u32[]{:S(2)}) %all-to-all-start.2) | async-done | bytes 1572896 | tf_op jit(solution)/shard_map/all_to_all | solution.py:85
  411.7 7.4 %all-to-all-start.4 = ((bf16[64,96,128]{2,1,0:T(8,128)(2,1)}), bf16[64,96,128]{2,1,0:T(8,128)(2,1)S(1)}, u32[]{:S(2)}, u32[]{:S(2)}) async-start(bf16[64,96,128]{2,1,0:T(8,128)(2,1)} %bitcast.43), calls=%async_computation.4 | async-start | bytes 3145728 | tf_op jit(solution)/shard_map/all_to_all | solution.py:86
  420.7 36.7 %all-to-all-done.4 = bf16[64,96,128]{2,1,0:T(8,128)(2,1)S(1)} async-done(((bf16[64,96,128]{2,1,0:T(8,128)(2,1)}), bf16[64,96,128]{2,1,0:T(8,128)(2,1)S(1)}, u32[]{:S(2)}, u32[]{:S(2)}) %all-to-all-start.4) | async-done | bytes 1572896 | tf_op jit(solution)/shard_map/all_to_all | solution.py:86
  457.4 27.1 %while.51 = (s32[]{:T(128)}, f32[1,256]{1,0:T(1,128)S(1)}, f32[1,256]{1,0:T(1,128)S(1)}, f32[1,256,128]{2,1,0:T(8,128)S(1)}, s32[]{:T(128)}, /*index=5*/s32[256]...) while((s32[]{:T(128)}, f32[1,256]{1,0:T(1,128)S(1)}, ...), condition=%wide.region_11.12_spmd, body=%wide.region_6.11_spmd.sunk | while | flops 68748288 | bytes 2190645 | solution.py:140
  458.0 1.8 conditional.6
  460.4 1.8 conditional.6
  462.8 1.8 conditional.6
  465.2 1.8 conditional.6
  467.6 1.8 conditional.6
  470.0 1.8 conditional.6
  472.5 1.8 conditional.6
  474.9 1.8 conditional.6
  477.3 1.8 conditional.6
  479.7 1.8 conditional.6
  482.1 1.8 conditional.6
  484.6 30.5 %while.52 = (s32[]{:T(128)}, f32[1,256]{1,0:T(1,128)S(1)}, f32[1,256]{1,0:T(1,128)S(1)}, f32[1,256,128]{2,1,0:T(8,128)S(1)}, s32[]{:T(128)}, /*index=5*/s32[256]...) while((s32[]{:T(128)}, f32[1,256]{1,0:T(1,128)S(1)}, ...), condition=%wide.region_18.19_spmd, body=%wide.region_13.18_spmd.sunk | while | flops 68748288 | bytes 2190645 | solution.py:140
  485.3 1.8 conditional.7
  487.8 1.8 conditional.7
  490.4 1.8 conditional.7
  492.9 1.8 conditional.7
  495.5 1.8 conditional.7
  498.0 1.8 conditional.7
  500.5 1.8 conditional.7
  503.1 1.8 conditional.7
  505.6 1.8 conditional.7
  508.2 1.8 conditional.7
  510.7 1.8 conditional.7
  513.2 1.8 conditional.7
  515.1 30.0 %while.53 = (s32[]{:T(128)}, f32[1,256]{1,0:T(1,128)S(1)}, f32[1,256]{1,0:T(1,128)S(1)}, f32[1,256,128]{2,1,0:T(8,128)S(1)}, s32[]{:T(128)}, /*index=5*/s32[256]...) while((s32[]{:T(128)}, f32[1,256]{1,0:T(1,128)S(1)}, ...), condition=%wide.region_25.26_spmd, body=%wide.region_20.25_spmd.sunk | while | flops 68748288 | bytes 2190645 | solution.py:140
  515.8 1.8 conditional.8
  518.3 1.8 conditional.8
  520.8 1.8 conditional.8
  523.3 1.8 conditional.8
  525.8 1.8 conditional.8
  528.3 1.8 conditional.8
  530.8 1.8 conditional.8
  533.3 1.8 conditional.8
  535.8 1.8 conditional.8
  538.3 1.8 conditional.8
  540.8 1.8 conditional.8
  543.3 1.8 conditional.8
  (319 shorter events, 80.0 us)
Async XLA Ops:
  8.7 26.6 %all-to-all-start = ((s32[64,2,96]{2,1,0:T(2,128)}), s32[64,2,96]{2,1,0:T(2,128)S(1)}, u32[]{:S(2)}, u32[]{:S(2)}) async-start(s32[64,2,96]{2,1,0:T(2,128)} %stack.2), calls=%async_computation | async-start | bytes 131072 | tf_op jit(solution)/shard_map/all_to_all | solution.py:45
  24.7 157.6 %all-reduce.2.cloned.1.call-start = ((), (), s32[]{:S(2)}) async-start(), calls=%async_computation.5 | async-start | bytes 6291456 | tf_op jit(solution)/shard_map/psum | solution.py:52
  104.8 163.2 %all-gather.3.cloned.1.call-start = ((), (), s32[]{:S(2)}) async-start(), calls=%async_computation.6 | async-start | bytes 6389760 | tf_op jit(solution)/shard_map/all_gather | solution.py:58
  190.2 53.9 %all-to-all-start.1 = ((bf16[64,2,6144]{2,1,0:T(2,128)(2,1)}), bf16[64,2,6144]{2,1,0:T(2,128)(2,1)S(1)}, u32[]{:S(2)}, u32[]{:S(2)}) async-start(bf16[64,2,6144]{2,1,0:T(2,128)(2,1)} %reshape.311), calls=%async_computation.1 | async-start | bytes 3145728 | tf_op jit(solution)/shard_map/all_to_all | solution.py:53
  203.0 96.4 %all-gather.5.cloned.1.call-start = ((), (), s32[]{:S(2)}) async-start(), calls=%async_computation.7 | async-start | bytes 2654208 | tf_op jit(solution)/shard_map/all_gather | solution.py:61
  264.0 1.4 copy-start.1
  301.6 1.7 copy-start
  303.3 0.7 copy-start.2
  309.1 13.8 %copy-start.3 = (f32[128]{0:T(128)S(1)}, f32[128]{0:T(128)}, u32[]{:S(2)}) copy-start(f32[128]{0:T(128)} %param.23) | copy-start | bytes 1540
  309.1 52.9 %all-to-all-start.3 = ((bf16[64,96,128]{2,1,0:T(8,128)(2,1)}), bf16[64,96,128]{2,1,0:T(8,128)(2,1)}, u32[]{:S(2)}, u32[]{:S(2)}) async-start(bf16[64,96,128]{2,1,0:T(8,128)(2,1)} %bitcast.170), calls=%async_computation.3 | async-start | bytes 3145728 | tf_op jit(solution)/shard_map/all_to_all | solution.py:84
  324.1 47.7 %slice-start = ((bf16[2,96,6144]{2,1,0:T(8,128)(2,1)}), bf16[2,96,1024]{2,1,0:T(8,128)(2,1)S(1)}, s32[]{:S(2)}) async-start(bf16[2,96,6144]{2,1,0:T(8,128)(2,1)} %all-gather.5.cloned.1.call-done), calls=%async_computation.8 | async-start | bytes 786432 | tf_op jit(solution)/shard_map/slice | solution.py:74
  363.4 46.9 %all-to-all-start.2 = ((bf16[64,96,128]{2,1,0:T(8,128)(2,1)}), bf16[64,96,128]{2,1,0:T(8,128)(2,1)}, u32[]{:S(2)}, u32[]{:S(2)}) async-start(bf16[64,96,128]{2,1,0:T(8,128)(2,1)} %bitcast.169), calls=%async_computation.2 | async-start | bytes 3145728 | tf_op jit(solution)/shard_map/all_to_all | solution.py:85
  411.7 45.7 %all-to-all-start.4 = ((bf16[64,96,128]{2,1,0:T(8,128)(2,1)}), bf16[64,96,128]{2,1,0:T(8,128)(2,1)S(1)}, u32[]{:S(2)}, u32[]{:S(2)}) async-start(bf16[64,96,128]{2,1,0:T(8,128)(2,1)} %bitcast.43), calls=%async_computation.4 | async-start | bytes 3145728 | tf_op jit(solution)/shard_map/all_to_all | solution.py:86
Sparse Core Ops, SparseCore 0:
  105.0 77.3 all-reduce.1
  273.1 26.1 all-gather.4
Sparse Core Ops, SparseCore 1:
  108.3 84.4 all-gather.2
